TPU v7x, 32 devices: a whole 2x2x4 slice. The times are simulated.
32 devices in a mesh: batch: 2 (over y), row: 4 (over x, core), col: 4 (over z).
Axes of the slice: x: 2, y: 2, z: 4, core: 2. Of those that a mesh axis runs over, the one named last changes fastest.
Arguments:
- patches: bfloat16 [2, 4096, 1280], P('batch', 'col', 'row'), may hold values from -6 to 6
- qkv_weight: bfloat16 [1280, 3, 1280], P('row', None, 'col'), may hold values from -0.15625 to 0.15625
- qv_bias: float32 [2, 1280], P(None, 'col'), may hold values from -0.6 to 0.6
- proj_weight: bfloat16 [1280, 1280], P('col', 'row'), may hold values from -2.5 to 2.5
- proj_bias: float32 [1280], P('row'), may hold values from -1.2 to 1.2
- norm1_gain: float32 [1280], P('row'), may hold values from 0.5 to 1.5
- norm1_shift: float32 [1280], P('row'), may hold values from -1.2 to 1.2
- norm2_gain: float32 [1280], P('row'), may hold values from 0.5 to 1.5
- norm2_shift: float32 [1280], P('row'), may hold values from -1.2 to 1.2
- fc1_weight: bfloat16 [1280, 5120], P('row', 'col'), may hold values from -0.15625 to 0.15625
- fc1_bias: float32 [5120], P('col'), may hold values from -1.2 to 1.2
- fc2_weight: bfloat16 [5120, 1280], P('col', 'row'), may hold values from -0.078125 to 0.078125
- fc2_bias: float32 [1280], P('row'), may hold values from -1.2 to 1.2
- height_table: bfloat16 [127, 80], replicated, may hold values from -0.625 to 0.625
- width_table: bfloat16 [127, 80], replicated, may hold values from -0.625 to 0.625
- out_grad: bfloat16 [2, 4096, 1280], P('batch', 'col', 'row'), may hold values from -6 to 6
Outputs:
- block_out: bfloat16 [2, 4096, 1280], P('batch', 'col', 'row')
- patches_grad: float32 [2, 4096, 1280], P('batch', 'col', 'row')
- qkv_weight_grad: float32 [1280, 3, 1280], P('row', None, 'col')
- qv_bias_grad: float32 [2, 1280], P(None, 'col')
- proj_weight_grad: float32 [1280, 1280], P('col', 'row')
- proj_bias_grad: float32 [1280], P('row')
- norm1_gain_grad: float32 [1280], P('row')
- norm1_shift_grad: float32 [1280], P('row')
- norm2_gain_grad: float32 [1280], P('row')
- norm2_shift_grad: float32 [1280], P('row')
- fc1_weight_grad: float32 [1280, 5120], P('row', 'col')
- fc1_bias_grad: float32 [5120], P('col')
- fc2_weight_grad: float32 [5120, 1280], P('col', 'row')
- fc2_bias_grad: float32 [1280], P('row')
- height_table_grad: float32 [127, 80], replicated
- width_table_grad: float32 [127, 80], replicated
All inputs are finite; a program needn't handle non-finite values.
Results may differ from a plain program's by a relative error of at most 0.012.
Values may be sent and summed in bfloat16 or wider, within the bound.
A program may use at most 256 MiB of HBM per device.

v0:
```python
from functools import partial
import jax
import jax.numpy as jnp
from jax import lax
from jax.sharding import PartitionSpec as P

D = 1280
HEAD_DIM = 80
GRID = 64
EPSILON = 1e-06
HIGHEST = lax.Precision.HIGHEST


def feature_sums(first, second):
    return lax.psum((first, second), "row")


def rows_over_col(values):
    return lax.all_gather(values, "col", axis=0, tiled=True)


def rows_over_row(values):
    return lax.all_gather(values, "row", axis=0, tiled=True)


def sum_over_row(values):
    return lax.psum_scatter(values, "row", scatter_dimension=0, tiled=True)


def sum_over_col(values):
    return lax.psum_scatter(values, "col", scatter_dimension=0, tiled=True)


def gather_key_value(key_local, value_local):
    couple = jnp.stack([key_local, value_local], 1).astype(jnp.bfloat16)
    couple_full = lax.all_gather(couple, "row", axis=0, tiled=True)
    return (couple_full[:, 0], couple_full[:, 1])


def normalize(values, norm_gain, norm_shift, model_width):
    first, second = feature_sums(jnp.sum(values, -1), jnp.sum(values * values, -1))
    center = first / model_width
    inv_scale = lax.rsqrt(second / model_width - center * center + EPSILON)
    scaled = (values - center[:, None]) * inv_scale[:, None]
    return (scaled, inv_scale, (scaled * norm_gain + norm_shift).astype(jnp.bfloat16))


def normalize_back(grad_in, scaled, inv_scale, norm_gain, model_width):
    scaled_grad = grad_in * norm_gain
    first, second = feature_sums(jnp.sum(scaled_grad, -1), jnp.sum(scaled_grad * scaled, -1))
    return inv_scale[:, None] * (
        scaled_grad - first[:, None] / model_width - scaled * (second[:, None] / model_width)
    )


def select_table(row_count, col_count, offset, grid_side):
    shape = (row_count, col_count, 2 * grid_side - 1)
    first = lax.broadcasted_iota(jnp.int32, shape, 0) + offset
    second = lax.broadcasted_iota(jnp.int32, shape, 1)
    third = lax.broadcasted_iota(jnp.int32, shape, 2)
    return (first - second + grid_side - 1 == third).astype(jnp.bfloat16)


def head_scores(query_one, key_one, row_select, col_select, score_scale, grid_side):
    query_lines = query_one.shape[0] // grid_side
    query_grid = query_one.reshape(query_lines, grid_side, query_one.shape[1])
    rel_rows = jnp.einsum(
        "hwc,hkc->hwk", query_grid, row_select, preferred_element_type=jnp.float32
    )
    rel_cols = jnp.einsum(
        "hwc,wkc->hwk", query_grid, col_select, preferred_element_type=jnp.float32
    )
    position = (rel_rows[:, :, :, None] + rel_cols[:, :, None, :]).reshape(
        query_one.shape[0], grid_side * grid_side
    )
    raw = jnp.einsum("qc,kc->qk", query_one, key_one, preferred_element_type=jnp.float32)
    return raw * score_scale + position


def shards(
    patches,
    qkv_weight,
    qv_bias,
    proj_weight,
    proj_bias,
    norm1_gain,
    norm1_shift,
    norm2_gain,
    norm2_shift,
    fc1_weight,
    fc1_bias,
    fc2_weight,
    fc2_bias,
    height_table,
    width_table,
    out_grad,
):
    grid_side = GRID
    model_width = D
    head_size = HEAD_DIM
    score_scale = head_size ** (-0.5)
    local_cols = qkv_weight.shape[2]
    head_count = local_cols // head_size
    image_tokens = grid_side * grid_side
    query_rows = image_tokens // lax.axis_size("row")
    query_lines = query_rows // grid_side
    residual = patches[0].astype(jnp.float32)
    scaled1, inv_scale1, normed1 = normalize(residual, norm1_gain, norm1_shift, model_width)
    gathered1 = rows_over_col(normed1)
    partial_qkv = jnp.einsum(
        "lf,fkh->lkh", gathered1, qkv_weight, preferred_element_type=jnp.float32
    )
    local_qkv = sum_over_row(partial_qkv)
    queries = local_qkv[:, 0] + qv_bias[0]
    key_full, value_full = gather_key_value(local_qkv[:, 1], local_qkv[:, 2] + qv_bias[1])
    queries = queries.astype(jnp.bfloat16)
    row_onehot = select_table(
        query_lines, grid_side, lax.axis_index("row") * query_lines, grid_side
    )
    col_onehot = select_table(grid_side, grid_side, 0, grid_side)
    row_select = jnp.einsum(
        "ijd,dc->ijc", row_onehot, height_table, preferred_element_type=jnp.float32
    ).astype(jnp.bfloat16)
    col_select = jnp.einsum(
        "ijd,dc->ijc", col_onehot, width_table, preferred_element_type=jnp.float32
    ).astype(jnp.bfloat16)

    def split_heads(values):
        return values.reshape(values.shape[0], head_count, head_size).transpose(1, 0, 2)

    def join_heads(values):
        return values.transpose(1, 0, 2).reshape(values.shape[1], head_count * head_size)

    query_heads = split_heads(queries)
    key_heads = split_heads(key_full)
    value_heads = split_heads(value_full)

    def attend(operands):
        query_one, key_one, value_one = operands
        scores = head_scores(query_one, key_one, row_select, col_select, score_scale, grid_side)
        row_max = jnp.max(scores, -1, keepdims=True)
        raw_weights = jnp.exp(scores - row_max)
        row_total = jnp.sum(raw_weights, -1, keepdims=True)
        weights = (raw_weights / row_total).astype(jnp.bfloat16)
        result = jnp.dot(weights, value_one, preferred_element_type=jnp.float32).astype(
            jnp.bfloat16
        )
        return (result, (row_max + jnp.log(row_total))[:, 0])

    attended, log_total = lax.map(attend, (query_heads, key_heads, value_heads))
    merged = join_heads(attended)
    gathered_attn = rows_over_row(merged)
    projected = sum_over_col(
        jnp.dot(gathered_attn, proj_weight, preferred_element_type=jnp.float32)
    )
    middle = residual + (projected + proj_bias)
    scaled2, inv_scale2, normed2 = normalize(middle, norm2_gain, norm2_shift, model_width)
    gathered2 = rows_over_col(normed2)
    preact = (
        sum_over_row(jnp.dot(gathered2, fc1_weight, preferred_element_type=jnp.float32)) + fc1_bias
    )
    activated = jax.nn.gelu(preact, approximate=False).astype(jnp.bfloat16)
    gathered_act = rows_over_row(activated)
    lowered = sum_over_col(jnp.dot(gathered_act, fc2_weight, preferred_element_type=jnp.float32))
    final = middle + (lowered + fc2_bias)
    cotangent = out_grad[0]
    cot_all = rows_over_col(cotangent)
    fc2_grad, fc2_bias_grad = (
        jnp.einsum("lh,lf->hf", gathered_act, cot_all, preferred_element_type=jnp.float32),
        jnp.sum(cot_all, 0, dtype=jnp.float32),
    )
    act_grad = sum_over_row(
        jnp.einsum("lf,hf->lh", cot_all, fc2_weight, preferred_element_type=jnp.float32)
    )
    gelu_fn = partial(jax.nn.gelu, approximate=False)
    unused, gelu_back = jax.vjp(gelu_fn, preact)
    preact_grad = gelu_back(act_grad)[0].astype(jnp.bfloat16)
    preact_all = rows_over_row(preact_grad)
    fc1_grad, fc1_bias_grad = (
        jnp.einsum("lf,lh->fh", gathered2, preact_all, preferred_element_type=jnp.float32),
        jnp.sum(preact_all, 0, dtype=jnp.float32),
    )
    normed2_grad = sum_over_col(
        jnp.einsum("lh,fh->lf", preact_all, fc1_weight, preferred_element_type=jnp.float32)
    )
    gain2_part = jnp.sum(normed2_grad * scaled2, 0)
    shift2_part = jnp.sum(normed2_grad, 0)
    middle_grad = cotangent.astype(jnp.float32) + normalize_back(
        normed2_grad, scaled2, inv_scale2, norm2_gain, model_width
    )
    branch_grad = middle_grad.astype(jnp.bfloat16)
    branch_all = rows_over_col(branch_grad)
    proj_grad, proj_bias_grad = (
        jnp.einsum("lh,lf->hf", gathered_attn, branch_all, preferred_element_type=jnp.float32),
        jnp.sum(branch_all, 0, dtype=jnp.float32),
    )
    merged_grad = sum_over_row(
        jnp.einsum("lf,hf->lh", branch_all, proj_weight, preferred_element_type=jnp.float32)
    ).astype(jnp.bfloat16)
    merged_grad_heads = split_heads(merged_grad)

    def attend_back(operands):
        query_one, key_one, value_one, grad_one, total_one = operands
        scores = head_scores(query_one, key_one, row_select, col_select, score_scale, grid_side)
        weights = jnp.exp(scores - total_one[:, None])
        weight_grad = jnp.einsum(
            "qc,kc->qk", grad_one, value_one, preferred_element_type=jnp.float32
        )
        row_inner = jnp.sum(weights * weight_grad, -1, keepdims=True)
        score_grad = (weights * (weight_grad - row_inner)).astype(jnp.bfloat16)
        value_part = jnp.einsum(
            "qk,qc->kc", weights.astype(jnp.bfloat16), grad_one, preferred_element_type=jnp.float32
        )
        key_part = (
            jnp.einsum("qk,qc->kc", score_grad, query_one, preferred_element_type=jnp.float32)
            * score_scale
        )
        query_part = jnp.dot(score_grad, key_one, preferred_element_type=jnp.float32) * score_scale
        grid_form = score_grad.astype(jnp.float32).reshape(
            query_lines, grid_side, grid_side, grid_side
        )
        row_grad = jnp.sum(grid_form, 3)
        col_grad = jnp.sum(grid_form, 2)
        query_grid = query_one.astype(jnp.float32).reshape(query_lines, grid_side, head_size)
        from_rows = jnp.einsum(
            "hwk,hkc->hwc", row_grad, row_select.astype(jnp.float32), precision=HIGHEST
        )
        from_cols = jnp.einsum(
            "hwk,wkc->hwc", col_grad, col_select.astype(jnp.float32), precision=HIGHEST
        )
        query_part = query_part + (from_rows + from_cols).reshape(query_rows, head_size)
        row_select_grad = jnp.einsum("hwk,hwc->hkc", row_grad, query_grid, precision=HIGHEST)
        col_select_grad = jnp.einsum("hwk,hwc->wkc", col_grad, query_grid, precision=HIGHEST)
        return (query_part, key_part, value_part, row_select_grad, col_select_grad)

    query_parts, key_parts, value_parts, row_sel_grads, col_sel_grads = lax.map(
        attend_back, (query_heads, key_heads, value_heads, merged_grad_heads, log_total)
    )
    kv_grad = sum_over_row(jnp.stack([join_heads(key_parts), join_heads(value_parts)], 1)).astype(
        jnp.bfloat16
    )
    query_grad = join_heads(query_parts).astype(jnp.bfloat16)
    qkv_grad_local = jnp.concatenate([query_grad[:, None], kv_grad], 1)
    qkv_all = rows_over_row(qkv_grad_local)
    qkv_grad, qv_bias_grad = (
        jnp.einsum("lf,lkh->fkh", gathered1, qkv_all, preferred_element_type=jnp.float32),
        jnp.stack(
            [
                jnp.sum(qkv_all[:, 0], 0, dtype=jnp.float32),
                jnp.sum(qkv_all[:, 2], 0, dtype=jnp.float32),
            ],
            0,
        ),
    )
    normed1_grad = sum_over_col(
        jnp.einsum("lkh,fkh->lf", qkv_all, qkv_weight, preferred_element_type=jnp.float32)
    )
    gain1_part = jnp.sum(normed1_grad * scaled1, 0)
    shift1_part = jnp.sum(normed1_grad, 0)
    input_grad = middle_grad + normalize_back(
        normed1_grad, scaled1, inv_scale1, norm1_gain, model_width
    )
    height_part = jnp.einsum(
        "ijd,ijc->dc", row_onehot.astype(jnp.float32), jnp.sum(row_sel_grads, 0), precision=HIGHEST
    )
    width_part = jnp.einsum(
        "ijd,ijc->dc", col_onehot.astype(jnp.float32), jnp.sum(col_sel_grads, 0), precision=HIGHEST
    )
    gain1_grad, shift1_grad, gain2_grad, shift2_grad = lax.psum(
        (gain1_part, shift1_part, gain2_part, shift2_part), ("batch", "col")
    )
    height_grad, width_grad = lax.psum((height_part, width_part), ("batch", "row", "col"))
    (
        qkv_grad,
        qv_bias_grad,
        proj_grad,
        proj_bias_grad,
        fc1_grad,
        fc1_bias_grad,
        fc2_grad,
        fc2_bias_grad,
    ) = (
        lax.psum(qkv_grad.astype(jnp.bfloat16), "batch").astype(jnp.float32),
        lax.psum(qv_bias_grad.astype(jnp.bfloat16), "batch").astype(jnp.float32),
        lax.psum(proj_grad.astype(jnp.bfloat16), "batch").astype(jnp.float32),
        lax.psum(proj_bias_grad.astype(jnp.bfloat16), "batch").astype(jnp.float32),
        lax.psum(fc1_grad.astype(jnp.bfloat16), "batch").astype(jnp.float32),
        lax.psum(fc1_bias_grad.astype(jnp.bfloat16), "batch").astype(jnp.float32),
        lax.psum(fc2_grad.astype(jnp.bfloat16), "batch").astype(jnp.float32),
        lax.psum(fc2_bias_grad.astype(jnp.bfloat16), "batch").astype(jnp.float32),
    )
    return (
        final[None].astype(jnp.bfloat16),
        input_grad[None],
        qkv_grad,
        qv_bias_grad,
        proj_grad,
        proj_bias_grad,
        gain1_grad,
        shift1_grad,
        gain2_grad,
        shift2_grad,
        fc1_grad,
        fc1_bias_grad,
        fc2_grad,
        fc2_bias_grad,
        height_grad,
        width_grad,
    )


def solution(mesh):
    in_specs = (
        P("batch", "col", "row"),
        P("row", None, "col"),
        P(None, "col"),
        P("col", "row"),
        P("row"),
        P("row"),
        P("row"),
        P("row"),
        P("row"),
        P("row", "col"),
        P("col"),
        P("col", "row"),
        P("row"),
        P(),
        P(),
        P("batch", "col", "row"),
    )
    out_specs = (
        P("batch", "col", "row"),
        P("batch", "col", "row"),
        P("row", None, "col"),
        P(None, "col"),
        P("col", "row"),
        P("row"),
        P("row"),
        P("row"),
        P("row"),
        P("row"),
        P("row", "col"),
        P("col"),
        P("col", "row"),
        P("row"),
        P(),
        P(),
    )
    return jax.shard_map(shards, mesh=mesh, in_specs=in_specs, out_specs=out_specs, check_vma=False)
```

profile of v0, /device:TPU:8, one launch (start us, length us, event | category | flops | bytes accessed | tf_op | source)
XLA Modules:
  0.0 2642.6 jit_solution(13296211281150519857)
XLA Ops:
  19.7 53.3 %all-gather.11.cloned.1.call-done = bf16[4096,320]{0,1:T(8,128)(2,1)} async-done(((bf16[1024,320]{0,1:T(8,128)(2,1)}), bf16[4096,320]{0,1:T(8,128)(2,1)}) %all-gather.11.cloned.1.call-update) | async-done | bytes 2621456 | tf_op jit(solution)/shard_map/all_gather | solution.py:19
  73.0 11.7 fusion.60
  85.4 119.9 %reduce-scatter.10.cloned.1.call-done = f32[1024,3,320]{0,2,1:T(8,128)} async-done(((f32[4096,3,320]{0,2,1:T(8,128)}), f32[1024,3,320]{0,2,1:T(8,128)}) %reduce-scatter.10.cloned.1.call-update) | async-done | bytes 3932176 | tf_op jit(solution)/shard_map/reduce_scatter | solution.py:27
  218.2 33.4 %all-gather.13.cloned.1.call-done = bf16[4096,2,320]{0,2,1:T(8,128)(2,1)} async-done(((bf16[1024,2,320]{0,2,1:T(8,128)(2,1)}), bf16[4096,2,320]{0,2,1:T(8,128)(2,1)}) %all-gather.13.cloned.1.call-update) | async-done | bytes 5242896 | tf_op jit(solution)/shard_map/all_gather | solution.py:36
  268.2 293.5 %while.30 = (s32[]{:T(128)}, bf16[4,1024,80]{1,2,0:T(8,128)(2,1)S(1)}, f32[4,1024]{1,0:T(4,128)}, bf16[4,1024,80]{2,1,0:T(8,128)(2,1)}, bf16[4,4096,80]{2,1,0:T(...) while((s32[]{:T(128)}, ...), condition=%wide.region_8.9_spmd, body=%wide.region_5.8_spmd.sunk | while | flops 1400978432 | bytes 123054200 | solution.py:150
  270.3 11.4 broadcast_add_fusion.4
  281.7 27.9 %add.329 = f32[1024,4096]{1,0:T(8,128)} reshape(f32[16,64,64,64]{3,2,1,0:T(8,128)} %broadcast_add_fusion.4) | data formatting | bytes 33554432 | tf_op jit(solution)/shard_map/while/body/eval_jaxpr/add | solution.py:73
  309.6 14.6 fusion.193
  343.6 11.4 broadcast_add_fusion.4
  355.1 27.9 %add.329 = f32[1024,4096]{1,0:T(8,128)} reshape(f32[16,64,64,64]{3,2,1,0:T(8,128)} %broadcast_add_fusion.4) | data formatting | bytes 33554432 | tf_op jit(solution)/shard_map/while/body/eval_jaxpr/add | solution.py:73
  383.0 14.6 fusion.193
  417.0 11.4 broadcast_add_fusion.4
  428.4 27.9 %add.329 = f32[1024,4096]{1,0:T(8,128)} reshape(f32[16,64,64,64]{3,2,1,0:T(8,128)} %broadcast_add_fusion.4) | data formatting | bytes 33554432 | tf_op jit(solution)/shard_map/while/body/eval_jaxpr/add | solution.py:73
  456.3 14.6 fusion.193
  490.4 11.4 broadcast_add_fusion.4
  501.8 27.9 %add.329 = f32[1024,4096]{1,0:T(8,128)} reshape(f32[16,64,64,64]{3,2,1,0:T(8,128)} %broadcast_add_fusion.4) | data formatting | bytes 33554432 | tf_op jit(solution)/shard_map/while/body/eval_jaxpr/add | solution.py:73
  529.7 14.6 fusion.193
  562.8 25.5 all-gather.15.cloned.1.call-done
  594.5 93.3 %reduce-scatter.12.cloned.1.call-done = f32[1024,320]{0,1:T(8,128)} async-done(((f32[4096,320]{0,1:T(8,128)}), f32[1024,320]{0,1:T(8,128)}) %reduce-scatter.12.cloned.1.call-update) | async-done | bytes 1310736 | tf_op jit(solution)/shard_map/reduce_scatter | solution.py:31
  700.1 42.7 %all-gather.27.cloned.1.call-done = bf16[1,4096,320]{1,2,0:T(8,128)(2,1)} async-done(((bf16[1,1024,320]{1,2,0:T(8,128)(2,1)}), bf16[1,4096,320]{1,2,0:T(8,128)(2,1)}) %all-gather.27.cloned.1.call-update) | async-done | bytes 2621456 | tf_op jit(solution)/shard_map/all_gather | solution.py:19
  742.8 11.7 fusion.56
  754.6 43.9 %all-gather.17.cloned.1.call-done = bf16[4096,320]{0,1:T(8,128)(2,1)} async-done(((bf16[1024,320]{0,1:T(8,128)(2,1)}), bf16[4096,320]{0,1:T(8,128)(2,1)}) %all-gather.17.cloned.1.call-update) | async-done | bytes 2621456 | tf_op jit(solution)/shard_map/all_gather | solution.py:19
  798.5 14.2 fusion.111
  812.8 142.1 %reduce-scatter.18.cloned.1.call-done = f32[1024,1280]{1,0:T(8,128)} async-done(((f32[4096,1280]{1,0:T(8,128)}), f32[1024,1280]{1,0:T(8,128)}) %reduce-scatter.18.cloned.1.call-update) | async-done | bytes 5242896 | tf_op jit(solution)/shard_map/reduce_scatter | solution.py:27
  954.9 155.9 %reduce-scatter.14.cloned.1.call-done = f32[1024,1280]{1,0:T(8,128)} async-done(((f32[4096,1280]{1,0:T(8,128)}), f32[1024,1280]{1,0:T(8,128)}) %reduce-scatter.14.cloned.1.call-update) | async-done | bytes 5242896 | tf_op jit(solution)/shard_map/reduce_scatter | solution.py:27
  1110.8 15.3 add_convert_fusion
  1126.2 70.3 %all-gather.21.cloned.1.call-done = bf16[4096,1280]{1,0:T(8,128)(2,1)} async-done(((bf16[1024,1280]{1,0:T(8,128)(2,1)}), bf16[4096,1280]{1,0:T(8,128)(2,1)}) %all-gather.21.cloned.1.call-update) | async-done | bytes 10485776 | tf_op jit(solution)/shard_map/all_gather | solution.py:23
  1196.5 12.6 fusion.113
  1209.2 93.9 %reduce-scatter.20.cloned.1.call-done = f32[1024,320]{0,1:T(8,128)} async-done(((f32[4096,320]{0,1:T(8,128)}), f32[1024,320]{0,1:T(8,128)}) %reduce-scatter.20.cloned.1.call-update) | async-done | bytes 1310736 | tf_op jit(solution)/shard_map/reduce_scatter | solution.py:31
  1316.0 52.7 %all-gather.23.cloned.1.call-done = bf16[4096,320]{0,1:T(8,128)(2,1)} async-done(((bf16[1024,320]{0,1:T(8,128)(2,1)}), bf16[4096,320]{0,1:T(8,128)(2,1)}) %all-gather.23.cloned.1.call-update) | async-done | bytes 2621456 | tf_op jit(solution)/shard_map/all_gather | solution.py:19
  1374.4 52.1 %reduce-scatter.22.cloned.1.call-done = f32[1024,320]{0,1:T(8,128)} async-done(((f32[4096,320]{0,1:T(8,128)}), f32[1024,320]{0,1:T(8,128)}) %reduce-scatter.22.cloned.1.call-update) | async-done | bytes 1310736 | tf_op jit(solution)/shard_map/reduce_scatter | solution.py:27
  1429.1 574.5 %while.31 = (s32[]{:T(128)}, bf16[4,1024,80]{1,2,0:T(8,128)(2,1)}, f32[4,4096,80]{1,2,0:T(8,128)}, f32[4,4096,80]{1,2,0:T(8,128)}, f32[4,16,64,80]{3,2,1,0:T(8,1...) while((s32[]{:T(128)}, bf16[4,1024,80]{1,2,0:T(8,128)(2,1)}, ...), condition=%wide.region_27.28_spmd, body=%wide.region_23.27_spmd.sunk | while | flops 3678845952 | bytes 353068224 | solution.py:236
  1441.7 11.3 broadcast_add_fusion.5
  1453.0 27.9 %add.336 = f32[1024,4096]{1,0:T(8,128)} reshape(f32[16,64,64,64]{3,2,1,0:T(8,128)} %broadcast_add_fusion.5) | data formatting | bytes 33554432 | tf_op jit(solution)/shard_map/while/body/eval_jaxpr/add | solution.py:73
  1480.9 16.5 multiply_reduce_fusion.7
  1497.4 11.9 multiply_convert_fusion.3
  1520.3 24.0 reshape.157
  1544.3 15.4 fusion.218
  1585.3 11.3 broadcast_add_fusion.5
  1596.6 27.9 %add.336 = f32[1024,4096]{1,0:T(8,128)} reshape(f32[16,64,64,64]{3,2,1,0:T(8,128)} %broadcast_add_fusion.5) | data formatting | bytes 33554432 | tf_op jit(solution)/shard_map/while/body/eval_jaxpr/add | solution.py:73
  1624.5 16.5 multiply_reduce_fusion.7
  1641.0 11.9 multiply_convert_fusion.3
  1663.8 24.0 reshape.157
  1687.8 15.4 fusion.218
  1740.1 27.9 %add.336 = f32[1024,4096]{1,0:T(8,128)} reshape(f32[16,64,64,64]{3,2,1,0:T(8,128)} %broadcast_add_fusion.5) | data formatting | bytes 33554432 | tf_op jit(solution)/shard_map/while/body/eval_jaxpr/add | solution.py:73
  1768.0 16.5 multiply_reduce_fusion.7
  1784.5 11.9 multiply_convert_fusion.3
  1807.3 24.0 reshape.157
  1831.3 15.4 fusion.218
  1872.2 11.3 broadcast_add_fusion.5
  1883.5 27.9 %add.336 = f32[1024,4096]{1,0:T(8,128)} reshape(f32[16,64,64,64]{3,2,1,0:T(8,128)} %broadcast_add_fusion.5) | data formatting | bytes 33554432 | tf_op jit(solution)/shard_map/while/body/eval_jaxpr/add | solution.py:73
  1911.4 16.5 multiply_reduce_fusion.7
  1927.9 11.9 multiply_convert_fusion.3
  1950.7 24.0 reshape.157
  1974.7 15.4 fusion.218
  2019.9 78.4 %reduce-scatter.24.cloned.1.call-done = f32[1024,2,320]{0,2,1:T(8,128)} async-done(((f32[4096,2,320]{0,2,1:T(8,128)}), f32[1024,2,320]{0,2,1:T(8,128)}) %reduce-scatter.24.cloned.1.call-update) | async-done | bytes 2621456 | tf_op jit(solution)/shard_map/reduce_scatter | solution.py:27
  2111.5 58.5 %all-gather.19.cloned.1.call-done = bf16[4096,1280]{1,0:T(8,128)(2,1)} async-done(((bf16[1024,1280]{1,0:T(8,128)(2,1)}), bf16[4096,1280]{1,0:T(8,128)(2,1)}) %all-gather.19.cloned.1.call-update) | async-done | bytes 10485776 | tf_op jit(solution)/shard_map/all_gather | solution.py:23
  2179.6 47.3 %all-gather.25.cloned.1.call-done = bf16[4096,3,320]{0,2,1:T(8,128)(2,1)} async-done(((bf16[1024,3,320]{0,2,1:T(8,128)(2,1)}), bf16[4096,3,320]{0,2,1:T(8,128)(2,1)}) %all-gather.25.cloned.1.call-update) | async-done | bytes 7864336 | tf_op jit(solution)/shard_map/all_gather | solution.py:23
  2244.5 12.8 fusion.112
  2285.6 25.0 all-reduce.13.cloned.1.call-done
  2318.5 88.2 %reduce-scatter.26.cloned.1.call-done = f32[1024,320]{0,1:T(8,128)} async-done(((f32[4096,320]{0,1:T(8,128)}), f32[1024,320]{0,1:T(8,128)}) %reduce-scatter.26.cloned.1.call-update) | async-done | bytes 1310736 | tf_op jit(solution)/shard_map/reduce_scatter | solution.py:31
  2415.5 87.7 %reduce-scatter.16.cloned.1.call-done = f32[1024,320]{0,1:T(8,128)} async-done(((f32[4096,320]{0,1:T(8,128)}), f32[1024,320]{0,1:T(8,128)}) %reduce-scatter.16.cloned.1.call-update) | async-done | bytes 1310736 | tf_op jit(solution)/shard_map/reduce_scatter | solution.py:31
  2507.6 19.1 all-reduce.1
  2526.7 106.0 %all-reduce.11.cloned.1.call-done = (f32[127,80]{0,1:T(8,128)}, f32[127,80]{0,1:T(8,128)}) async-done(((f32[127,80]{0,1:T(8,128)}, f32[127,80]{0,1:T(8,128)}), (f32[127,80]{0,1:T(8,128)}, f32[127,80]{0,1:T(8,128)})) %all-reduce.11.cloned.1.call-update) | async-done | bytes 81296 | tf_op jit(solution)/shard_map/psum | solution.py:272
  (306 shorter events, 426.7 us)
Async XLA Ops:
  7.2 791.3 %copy-start = (bf16[320,1280]{1,0:T(8,128)(2,1)S(1)}, bf16[320,1280]{1,0:T(8,128)(2,1)}, u32[]{:S(2)}) copy-start(bf16[320,1280]{1,0:T(8,128)(2,1)} %param.29) | copy-start | bytes 2457604
  7.2 65.8 %all-gather.11.cloned.1.call-start = ((), (), s32[]{:S(2)}) async-start(), calls=%async_computation.9 | async-start | bytes 3276800 | tf_op jit(solution)/shard_map/all_gather | solution.py:19
  19.7 185.7 %reduce-scatter.10.cloned.1.call-start = ((), (), s32[]{:S(2)}) async-start(), calls=%async_computation.10 | async-start | bytes 19660800 | tf_op jit(solution)/shard_map/reduce_scatter | solution.py:27
  84.7 126.9 %copy-start.44 = (bf16[127,80]{0,1:T(8,128)(2,1)S(1)}, bf16[127,80]{0,1:T(8,128)(2,1)}, u32[]{:S(2)}) copy-start(bf16[127,80]{0,1:T(8,128)(2,1)} %param.33) | copy-start | bytes 60964
  84.7 127.2 %copy-start.45 = (bf16[127,80]{0,1:T(8,128)(2,1)S(1)}, bf16[127,80]{0,1:T(8,128)(2,1)}, u32[]{:S(2)}) copy-start(bf16[127,80]{0,1:T(8,128)(2,1)} %param.34) | copy-start | bytes 60964
  84.7 166.8 %all-gather.13.cloned.1.call-start = ((), (), s32[]{:S(2)}) async-start(), calls=%async_computation.11 | async-start | bytes 6553600 | tf_op jit(solution)/shard_map/all_gather | solution.py:36
  211.0 377.3 %all-gather.15.cloned.1.call-start = ((), (), s32[]{:S(2)}) async-start(), calls=%async_computation.12 | async-start | bytes 3276800 | tf_op jit(solution)/shard_map/all_gather | solution.py:23
  211.6 45.4 %copy-start.42 = (s32[16]{0:T(128)}, s32[16]{0:T(128)S(1)}, u32[]{:S(2)}) copy-start(s32[16]{0:T(128)S(1)} %iota_add_fusion) | copy-start | bytes 196
  268.2 320.1 %copy-start.13 = (bf16[320,320]{1,0:T(8,128)(2,1)S(1)}, bf16[320,320]{1,0:T(8,128)(2,1)}, u32[]{:S(2)}) copy-start(bf16[320,320]{1,0:T(8,128)(2,1)} %param.23) | copy-start | bytes 614404
  562.6 125.3 %reduce-scatter.12.cloned.1.call-start = ((), (), s32[]{:S(2)}) async-start(), calls=%async_computation.13 | async-start | bytes 6553600 | tf_op jit(solution)/shard_map/reduce_scatter | solution.py:31
  593.9 93.9 %copy-start.5 = (bf16[1,1024,320]{1,2,0:T(8,128)(2,1)S(1)}, bf16[1,1024,320]{1,2,0:T(8,128)(2,1)}, u32[]{:S(2)}) copy-start(bf16[1,1024,320]{1,2,0:T(8,128)(2,1)} %param.20) | copy-start | bytes 1966084
  593.9 94.0 %copy-start.40 = (f32[320]{0:T(512)S(1)}, f32[320]{0:T(512)}, u32[]{:S(2)}) copy-start(f32[320]{0:T(512)} %param.24) | copy-start | bytes 3844
  593.9 103.7 %copy-start.31 = (f32[320]{0:T(512)S(1)}, f32[320]{0:T(512)}, u32[]{:S(2)}) copy-start(f32[320]{0:T(512)} %param.27) | copy-start | bytes 3844
  593.9 103.7 %copy-start.41 = (f32[320]{0:T(512)S(1)}, f32[320]{0:T(512)}, u32[]{:S(2)}) copy-start(f32[320]{0:T(512)} %param.28) | copy-start | bytes 3844
  593.9 148.9 %all-gather.27.cloned.1.call-start = ((), (), s32[]{:S(2)}) async-start(), calls=%async_computation.26 | async-start | bytes 3276800 | tf_op jit(solution)/shard_map/all_gather | solution.py:19
  594.5 204.0 %all-gather.17.cloned.1.call-start = ((), (), s32[]{:S(2)}) async-start(), calls=%async_computation.14 | async-start | bytes 3276800 | tf_op jit(solution)/shard_map/all_gather | solution.py:19
  697.5 615.4 %copy-start.19 = (f32[1024]{0:T(1024)}, f32[1024]{0:T(1024)S(1)}, u32[]{:S(2)}) copy-start(f32[1024]{0:T(1024)S(1)} %get-tuple-element.230) | copy-start | bytes 12292
  697.5 615.4 %copy-start.21 = (f32[1024]{0:T(1024)}, f32[1024]{0:T(1024)S(1)}, u32[]{:S(2)}) copy-start(f32[1024]{0:T(1024)S(1)} %get-tuple-element.231) | copy-start | bytes 12292
  700.0 254.9 %reduce-scatter.18.cloned.1.call-start = ((), (), s32[]{:S(2)}) async-start(), calls=%async_computation.18 | async-start | bytes 26214400 | tf_op jit(solution)/shard_map/reduce_scatter | solution.py:27
  754.5 356.3 %reduce-scatter.14.cloned.1.call-start = ((), (), s32[]{:S(2)}) async-start(), calls=%async_computation.15 | async-start | bytes 26214400 | tf_op jit(solution)/shard_map/reduce_scatter | solution.py:27
  812.7 298.1 %copy-start.33 = (f32[1280]{0:T(1024)S(1)}, f32[1280]{0:T(1024)}, u32[]{:S(2)}) copy-start(f32[1280]{0:T(1024)} %param.30) | copy-start | bytes 15364
  812.7 383.8 %all-gather.21.cloned.1.call-start = ((), (), s32[]{:S(2)}) async-start(), calls=%async_computation.19 | async-start | bytes 13107200 | tf_op jit(solution)/shard_map/all_gather | solution.py:23
  1126.1 176.9 %reduce-scatter.20.cloned.1.call-start = ((), (), s32[]{:S(2)}) async-start(), calls=%async_computation.20 | async-start | bytes 6553600 | tf_op jit(solution)/shard_map/reduce_scatter | solution.py:31
  1209.1 103.8 %copy-start.10 = (bf16[1,1024,320]{1,2,0:T(8,128)(2,1)S(1)}, bf16[1,1024,320]{1,2,0:T(8,128)(2,1)}, u32[]{:S(2)}) copy-start(bf16[1,1024,320]{1,2,0:T(8,128)(2,1)} %param.35) | copy-start | bytes 1966084
  1209.1 159.5 %all-gather.23.cloned.1.call-start = ((), (), s32[]{:S(2)}) async-start(), calls=%async_computation.21 | async-start | bytes 3276800 | tf_op jit(solution)/shard_map/all_gather | solution.py:19
  1312.9 61.4 %copy-start.27 = (f32[1024]{0:T(1024)}, f32[1024]{0:T(1024)S(1)}, u32[]{:S(2)}) copy-start(f32[1024]{0:T(1024)S(1)} %get-tuple-element.234) | copy-start | bytes 12292
  1312.9 61.4 %copy-start.29 = (f32[1024]{0:T(1024)}, f32[1024]{0:T(1024)S(1)}, u32[]{:S(2)}) copy-start(f32[1024]{0:T(1024)S(1)} %get-tuple-element.235) | copy-start | bytes 12292
  1315.9 110.5 %reduce-scatter.22.cloned.1.call-start = ((), (), s32[]{:S(2)}) async-start(), calls=%async_computation.22 | async-start | bytes 6553600 | tf_op jit(solution)/shard_map/reduce_scatter | solution.py:27
  1374.3 724.1 %reduce-scatter.24.cloned.1.call-start = ((), (), s32[]{:S(2)}) async-start(), calls=%async_computation.23 | async-start | bytes 13107200 | tf_op jit(solution)/shard_map/reduce_scatter | solution.py:27
  1497.4 15.4 copy-start.2
  1641.0 15.4 copy-start.2
  1784.5 15.4 copy-start.2
  1799.9 3.8 copy-start.3
  1927.9 15.4 copy-start.2
  1943.3 3.8 copy-start.3
  2012.9 157.2 %all-gather.19.cloned.1.call-start = ((), (), s32[]{:S(2)}) async-start(), calls=%async_computation.16 | async-start | bytes 13107200 | tf_op jit(solution)/shard_map/all_gather | solution.py:23
  2019.9 80.4 %copy-start.18 = (bf16[4,1024,80]{1,2,0:T(8,128)(2,1)S(1)}, bf16[4,1024,80]{1,2,0:T(8,128)(2,1)}, u32[]{:S(2)}) copy-start(bf16[4,1024,80]{1,2,0:T(8,128)(2,1)} %get-tuple-element.132) | copy-start | bytes 1966084
  2019.9 207.0 %all-gather.25.cloned.1.call-start = ((), (), s32[]{:S(2)}) async-start(), calls=%async_computation.24 | async-start | bytes 9830400 | tf_op jit(solution)/shard_map/all_gather | solution.py:23
  2101.8 68.3 %copy-start.7 = (bf16[1,4096,320]{1,2,0:T(8,128)(2,1)S(1)}, bf16[1,4096,320]{1,2,0:T(8,128)(2,1)}, u32[]{:S(2)}) copy-start(bf16[1,4096,320]{1,2,0:T(8,128)(2,1)} %all-gather.27.cloned.1.call-done) | copy-start | bytes 7864324
  2101.8 208.8 %all-reduce.13.cloned.1.call-start = ((), (), s32[]{:S(2)}) async-start(), calls=%async_computation.28 | async-start | bytes 5242880 | tf_op jit(solution)/shard_map/psum | solution.py:283
  2170.1 7.3 copy-start.8
  2170.1 7.3 copy-start.12
  2179.6 55.8 %copy-start.16 = (bf16[320,3,320]{2,0,1:T(8,128)(2,1)S(1)}, bf16[320,3,320]{2,0,1:T(8,128)(2,1)}, u32[]{:S(2)}) copy-start(bf16[320,3,320]{2,0,1:T(8,128)(2,1)} %param.21) | copy-start | bytes 1843204
  2235.4 171.2 %reduce-scatter.26.cloned.1.call-start = ((), (), s32[]{:S(2)}) async-start(), calls=%async_computation.25 | async-start | bytes 6553600 | tf_op jit(solution)/shard_map/reduce_scatter | solution.py:31
  2243.4 259.8 %reduce-scatter.16.cloned.1.call-start = ((), (), s32[]{:S(2)}) async-start(), calls=%async_computation.17 | async-start | bytes 6553600 | tf_op jit(solution)/shard_map/reduce_scatter | solution.py:31
  2257.3 375.4 %all-reduce.11.cloned.1.call-start = ((), (), s32[]{:S(2)}) async-start(), calls=%async_computation.27 | async-start | bytes 163840 | tf_op jit(solution)/shard_map/psum | solution.py:272
  2257.8 5.7 copy-start.9
  2264.0 6.7 copy-start.43
  2277.9 128.8 %copy-start.6 = (bf16[1,1024,320]{1,2,0:T(8,128)(2,1)S(1)}, bf16[1,1024,320]{1,2,0:T(8,128)(2,1)}, u32[]{:S(2)}) copy-start(bf16[1,1024,320]{1,2,0:T(8,128)(2,1)} %param.20) | copy-start | bytes 1966084
  2277.9 128.8 %copy-start.24 = (f32[1024]{0:T(1024)S(1)}, f32[1024]{0:T(1024)}, u32[]{:S(2)}) copy-start(f32[1024]{0:T(1024)} %copy-done.23) | copy-start | bytes 12292
  2277.9 128.8 %copy-start.26 = (f32[1024]{0:T(1024)S(1)}, f32[1024]{0:T(1024)}, u32[]{:S(2)}) copy-start(f32[1024]{0:T(1024)} %copy-done.25) | copy-start | bytes 12292
  2277.9 128.7 %copy-start.35 = (f32[320]{0:T(512)S(1)}, f32[320]{0:T(512)}, u32[]{:S(2)}) copy-start(f32[320]{0:T(512)} %param.25) | copy-start | bytes 3844
  2277.9 225.3 %copy-start.4 = (f32[1024,320]{0,1:T(8,128)S(1)}, f32[1024,320]{0,1:T(8,128)}, u32[]{:S(2)}) copy-start(f32[1024,320]{0,1:T(8,128)} %get-tuple-element.219) | copy-start | bytes 3932164
  2277.9 225.3 %copy-start.11 = (bf16[1,1024,320]{1,2,0:T(8,128)(2,1)S(1)}, bf16[1,1024,320]{1,2,0:T(8,128)(2,1)}, u32[]{:S(2)}) copy-start(bf16[1,1024,320]{1,2,0:T(8,128)(2,1)} %param.35) | copy-start | bytes 1966084
  2277.9 225.3 %copy-start.20 = (f32[1024]{0:T(1024)S(1)}, f32[1024]{0:T(1024)}, u32[]{:S(2)}) copy-start(f32[1024]{0:T(1024)} %copy-done.19) | copy-start | bytes 12292
  2277.9 225.3 %copy-start.22 = (f32[1024]{0:T(1024)S(1)}, f32[1024]{0:T(1024)}, u32[]{:S(2)}) copy-start(f32[1024]{0:T(1024)} %copy-done.21) | copy-start | bytes 12292
  2277.9 225.3 %copy-start.28 = (f32[1024]{0:T(1024)S(1)}, f32[1024]{0:T(1024)}, u32[]{:S(2)}) copy-start(f32[1024]{0:T(1024)} %copy-done.27) | copy-start | bytes 12292
  2277.9 225.3 %copy-start.30 = (f32[1024]{0:T(1024)S(1)}, f32[1024]{0:T(1024)}, u32[]{:S(2)}) copy-start(f32[1024]{0:T(1024)} %copy-done.29) | copy-start | bytes 12292
  2278.0 225.3 %copy-start.32 = (f32[320]{0:T(512)S(1)}, f32[320]{0:T(512)}, u32[]{:S(2)}) copy-start(f32[320]{0:T(512)} %param.27) | copy-start | bytes 3844
  2278.0 225.3 %copy-start.39 = (f32[320]{0:T(512)S(1)}, f32[320]{0:T(512)}, u32[]{:S(2)}) copy-start(f32[320]{0:T(512)} %param.32) | copy-start | bytes 3844
  2310.6 6.6 copy-start.14
  2317.2 318.4 %copy-start.1 = (bf16[320,1280]{1,0:T(8,128)(2,1)S(1)}, bf16[320,1280]{1,0:T(8,128)(2,1)}, u32[]{:S(2)}) copy-start(bf16[320,1280]{1,0:T(8,128)(2,1)} %param.29) | copy-start | bytes 2457604
  2318.5 189.1 %copy-start.36 = (f32[320]{0:T(512)S(1)}, f32[320]{0:T(512)}, u32[]{:S(2)}) copy-start(f32[320]{0:T(512)} %get-tuple-element.141) | copy-start | bytes 3844
  2318.5 189.1 %copy-start.37 = (f32[320]{0:T(512)S(1)}, f32[320]{0:T(512)}, u32[]{:S(2)}) copy-start(f32[320]{0:T(512)} %get-tuple-element.147) | copy-start | bytes 3844
  (8 other events, 12.1 us)
Sparse Core Ops, SparseCore 0:
  19.8 53.1 all-gather.10
  84.8 120.4 reduce-scatter.9
  211.1 40.4 all-gather.12
  562.7 25.5 all-gather.14
  594.0 93.7 reduce-scatter.11
  689.2 53.4 all-gather.26
  744.9 53.5 all-gather.16
  801.1 153.7 reduce-scatter.17
  957.7 153.1 reduce-scatter.13
  1126.3 70.1 all-gather.20
  1209.3 93.7 reduce-scatter.19
  1316.1 52.5 all-gather.22
  1374.4 51.9 reduce-scatter.21
  2013.0 85.3 reduce-scatter.23
  2099.8 70.1 all-gather.18
  2171.6 55.3 all-gather.24
  2235.5 75.0 all-reduce.12
  2312.8 93.8 reduce-scatter.25
  2408.9 94.2 reduce-scatter.15
  2509.3 123.4 all-reduce.10
where the time goes:
time: 2660 us; the launch traced here: 2640 us
  waiting for transfers between devices  1470 us (55%)
  matrix products  398 us (15%)
  local copies, waits for them, and re-layouts  380 us (14%)
  other arithmetic  324 us (12%)
  blocking collectives  52.3 us (2%)
    reduce_scatter x5, waiting for transfers between devices, sum_over_row(): return lax.psum_scatter(values, 'row', scatter_dimension=0, tiled=True)  548 us
    reduce_scatter x4, waiting for transfers between devices, sum_over_col(): return lax.psum_scatter(values, 'col', scatter_dimension=0, tiled=True)  363 us
    add x8, local copies, waits for them, and re-layouts, head_scores(): rel_rows[:, :, :, None] + rel_cols[:, :, None, :]  223 us
    all_gather x4, waiting for transfers between devices, rows_over_row(): return lax.all_gather(values, 'row', axis=0, tiled=True)  202 us
    all_gather x4, waiting for transfers between devices, rows_over_col(): return lax.all_gather(values, 'col', axis=0, tiled=True)  193 us
    dot_general x8, matrix products, head_scores(): jnp.einsum('qc,kc->qk', query_one, key_one, preferred_element_type=jnp.fl...  124 us
    psum x1, waiting for transfers between devices, shards(): lax.psum((height_part, width_part), ('batch', 'row', 'col'))  106 us
    reshape x4, local copies, waits for them, and re-layouts, attend_back(): score_grad.astype(jnp.float32)  96.1 us
  transfers between devices with their start and end apart: 20, of which 20 were waited for; matrix products, arithmetic and copies ran while one was open for 5% of the time, Pallas kernels for 0%

commit v1 on v0

--- a/solution.py
+++ b/solution.py
@@ -16,7 +16,9 @@
 
 
 def rows_over_col(values):
-    return lax.all_gather(values, "col", axis=0, tiled=True)
+    return jnp.concatenate(
+        lax.all_to_all(jnp.stack([values] * lax.axis_size("col")), "col", 0, 0), axis=0
+    )
 
 
 def rows_over_row(values):

time: 2660 us -> 2620 us (0.985)
  waiting for transfers between devices: 1470 us -> 1110 us
  blocking collectives: 52.3 us -> 367 us
    all_to_all x0 -> x4, blocking collectives: none -> 316 us  [rows_over_col(): lax.all_to_all(jnp.stack([values] * lax.axis_size('col')), 'col', 0, 0)]
    all_gather x4 -> x0, waiting for transfers between devices: 193 us -> none  [rows_over_col(): return lax.all_gather(values, 'col', axis=0, tiled=True)]
    reduce_scatter x4, waiting for transfers between devices: 363 us -> 273 us  [sum_over_col(): return lax.psum_scatter(values, 'col', scatter_dimension=0, tiled=True)]
    reduce_scatter x5, waiting for transfers between devices: 548 us -> 476 us  [sum_over_row(): return lax.psum_scatter(values, 'row', scatter_dimension=0, tiled=True)]
  transfers between devices with their start and end apart: 20 -> 16, of which waited for: 20 -> 16; matrix products, arithmetic and copies ran while one was open for 5% -> 5% of each run, Pallas kernels for 0% -> 0%
where the time goes in v1:
time: 2620 us; the launch traced here: 2600 us
  waiting for transfers between devices  1110 us (42%)
  local copies, waits for them, and re-layouts  397 us (15%)
  matrix products  388 us (15%)
  blocking collectives  367 us (14%)
  other arithmetic  321 us (12%)
    reduce_scatter x5, waiting for transfers between devices, sum_over_row(): return lax.psum_scatter(values, 'row', scatter_dimension=0, tiled=True)  476 us
    all_to_all x4, blocking collectives, rows_over_col(): lax.all_to_all(jnp.stack([values] * lax.axis_size('col')), 'col', 0, 0)  316 us
    reduce_scatter x4, waiting for transfers between devices, sum_over_col(): return lax.psum_scatter(values, 'col', scatter_dimension=0, tiled=True)  273 us
    add x8, local copies, waits for them, and re-layouts, head_scores(): rel_rows[:, :, :, None] + rel_cols[:, :, None, :]  223 us
    all_gather x4, waiting for transfers between devices, rows_over_row(): return lax.all_gather(values, 'row', axis=0, tiled=True)  202 us
    dot_general x8, matrix products, head_scores(): jnp.einsum('qc,kc->qk', query_one, key_one, preferred_element_type=jnp.fl...  124 us
    psum x1, waiting for transfers between devices, shards(): lax.psum((height_part, width_part), ('batch', 'row', 'col'))  106 us
    reshape x4, local copies, waits for them, and re-layouts, attend_back(): score_grad.astype(jnp.float32)  95.9 us
  transfers between devices with their start and end apart: 16, of which 16 were waited for; matrix products, arithmetic and copies ran while one was open for 5% of the time, Pallas kernels for 0%

profile of v1, /device:TPU:8, one launch (start us, length us, event | category | flops | bytes accessed | tf_op | source)
XLA Modules:
  0.0 2604.5 jit_solution(461979296085874811)
XLA Ops:
  19.1 61.5 %all_to_all.20 = bf16[4,1024,320]{1,2,0:T(8,128)(2,1)S(1)} all-to-all(bf16[4,1024,320]{1,2,0:T(8,128)(2,1)S(1)} %stack.47), channel_id=1, replica_groups=mesh['batch'=2,'row'=4,'col'=4] {'col'}, dimensions={0} | all-to-all | bytes 5242880 | tf_op jit(solution)/shard_map/all_to_all | solution.py:20
  86.2 11.7 fusion.102
  98.6 119.8 %reduce-scatter.10.cloned.1.call-done = f32[1024,3,320]{0,2,1:T(8,128)} async-done(((f32[4096,3,320]{0,2,1:T(8,128)}), f32[1024,3,320]{0,2,1:T(8,128)}) %reduce-scatter.10.cloned.1.call-update) | async-done | bytes 3932176 | tf_op jit(solution)/shard_map/reduce_scatter | solution.py:29
  230.9 33.7 %all-gather.6.cloned.1.call-done = bf16[4096,2,320]{0,2,1:T(8,128)(2,1)} async-done(((bf16[1024,2,320]{0,2,1:T(8,128)(2,1)}), bf16[4096,2,320]{0,2,1:T(8,128)(2,1)}) %all-gather.6.cloned.1.call-update) | async-done | bytes 5242896 | tf_op jit(solution)/shard_map/all_gather | solution.py:38
  281.2 293.6 %while.30 = (s32[]{:T(128)}, bf16[4,1024,80]{1,2,0:T(8,128)(2,1)S(1)}, f32[4,1024]{1,0:T(4,128)}, bf16[4,1024,80]{2,1,0:T(8,128)(2,1)}, bf16[4,4096,80]{2,1,0:T(...) while((s32[]{:T(128)}, ...), condition=%wide.region_8.9_spmd, body=%wide.region_5.8_spmd.sunk | while | flops 1400978432 | bytes 123054200 | solution.py:152
  283.3 11.4 broadcast_add_fusion.4
  294.7 27.9 %add.332 = f32[1024,4096]{1,0:T(8,128)} reshape(f32[16,64,64,64]{3,2,1,0:T(8,128)} %broadcast_add_fusion.4) | data formatting | bytes 33554432 | tf_op jit(solution)/shard_map/while/body/eval_jaxpr/add | solution.py:75
  322.6 14.6 fusion.191
  356.7 11.4 broadcast_add_fusion.4
  368.1 27.9 %add.332 = f32[1024,4096]{1,0:T(8,128)} reshape(f32[16,64,64,64]{3,2,1,0:T(8,128)} %broadcast_add_fusion.4) | data formatting | bytes 33554432 | tf_op jit(solution)/shard_map/while/body/eval_jaxpr/add | solution.py:75
  396.0 14.6 fusion.191
  430.1 11.4 broadcast_add_fusion.4
  441.5 27.9 %add.332 = f32[1024,4096]{1,0:T(8,128)} reshape(f32[16,64,64,64]{3,2,1,0:T(8,128)} %broadcast_add_fusion.4) | data formatting | bytes 33554432 | tf_op jit(solution)/shard_map/while/body/eval_jaxpr/add | solution.py:75
  469.4 14.6 fusion.191
  503.5 11.4 broadcast_add_fusion.4
  514.9 27.9 %add.332 = f32[1024,4096]{1,0:T(8,128)} reshape(f32[16,64,64,64]{3,2,1,0:T(8,128)} %broadcast_add_fusion.4) | data formatting | bytes 33554432 | tf_op jit(solution)/shard_map/while/body/eval_jaxpr/add | solution.py:75
  542.8 14.6 fusion.191
  576.1 25.2 all-gather.8.cloned.1.call-done
  607.4 132.7 %all_to_all.21 = bf16[4,1024,320]{1,2,0:T(8,128)(2,1)S(1)} all-to-all(bf16[4,1024,320]{1,2,0:T(8,128)(2,1)S(1)} %stack.50), channel_id=1, replica_groups=mesh['batch'=2,'row'=4,'col'=4] {'col'}, dimensions={0} | all-to-all | bytes 5242880 | tf_op jit(solution)/shard_map/all_to_all | solution.py:20
  743.4 10.0 fusion.106
  767.6 60.4 %all_to_all.22 = bf16[4,1024,320]{1,2,0:T(8,128)(2,1)S(1)} all-to-all(bf16[4,1024,320]{1,2,0:T(8,128)(2,1)S(1)} %stack.49), channel_id=1, replica_groups=mesh['batch'=2,'row'=4,'col'=4] {'col'}, dimensions={0} | all-to-all | bytes 5242880 | tf_op jit(solution)/shard_map/all_to_all | solution.py:20
  829.9 9.9 fusion.104
  839.9 70.5 %reduce-scatter.18.cloned.1.call-done = f32[1024,1280]{1,0:T(8,128)} async-done(((f32[4096,1280]{1,0:T(8,128)}), f32[1024,1280]{1,0:T(8,128)}) %reduce-scatter.18.cloned.1.call-update) | async-done | bytes 5242896 | tf_op jit(solution)/shard_map/reduce_scatter | solution.py:29
  910.4 155.8 %reduce-scatter.14.cloned.1.call-done = f32[1024,1280]{1,0:T(8,128)} async-done(((f32[4096,1280]{1,0:T(8,128)}), f32[1024,1280]{1,0:T(8,128)}) %reduce-scatter.14.cloned.1.call-update) | async-done | bytes 5242896 | tf_op jit(solution)/shard_map/reduce_scatter | solution.py:29
  1066.2 15.2 add_convert_fusion
  1081.4 70.3 %all-gather.12.cloned.1.call-done = bf16[4096,1280]{1,0:T(8,128)(2,1)} async-done(((bf16[1024,1280]{1,0:T(8,128)(2,1)}), bf16[4096,1280]{1,0:T(8,128)(2,1)}) %all-gather.12.cloned.1.call-update) | async-done | bytes 10485776 | tf_op jit(solution)/shard_map/all_gather | solution.py:25
  1151.8 12.6 fusion.107
  1164.5 93.9 %reduce-scatter.20.cloned.1.call-done = f32[1024,320]{0,1:T(8,128)} async-done(((f32[4096,320]{0,1:T(8,128)}), f32[1024,320]{0,1:T(8,128)}) %reduce-scatter.20.cloned.1.call-update) | async-done | bytes 1310736 | tf_op jit(solution)/shard_map/reduce_scatter | solution.py:33
  1270.7 60.9 %all_to_all.23 = bf16[4,1024,320]{1,2,0:T(8,128)(2,1)S(1)} all-to-all(bf16[4,1024,320]{1,2,0:T(8,128)(2,1)S(1)} %stack.51), channel_id=1, replica_groups=mesh['batch'=2,'row'=4,'col'=4] {'col'}, dimensions={0} | all-to-all | bytes 5242880 | tf_op jit(solution)/shard_map/all_to_all | solution.py:20
  1338.9 51.8 %reduce-scatter.22.cloned.1.call-done = f32[1024,320]{0,1:T(8,128)} async-done(((f32[4096,320]{0,1:T(8,128)}), f32[1024,320]{0,1:T(8,128)}) %reduce-scatter.22.cloned.1.call-update) | async-done | bytes 1310736 | tf_op jit(solution)/shard_map/reduce_scatter | solution.py:29
  1393.4 574.2 %while.31 = (s32[]{:T(128)}, bf16[4,1024,80]{1,2,0:T(8,128)(2,1)}, f32[4,4096,80]{1,2,0:T(8,128)}, f32[4,4096,80]{1,2,0:T(8,128)}, f32[4,16,64,80]{3,2,1,0:T(8,1...) while((s32[]{:T(128)}, bf16[4,1024,80]{1,2,0:T(8,128)(2,1)}, ...), condition=%wide.region_27.28_spmd, body=%wide.region_23.27_spmd.sunk | while | flops 3678845952 | bytes 353068224 | solution.py:238
  1405.7 11.3 broadcast_add_fusion.5
  1417.1 27.9 %add.339 = f32[1024,4096]{1,0:T(8,128)} reshape(f32[16,64,64,64]{3,2,1,0:T(8,128)} %broadcast_add_fusion.5) | data formatting | bytes 33554432 | tf_op jit(solution)/shard_map/while/body/eval_jaxpr/add | solution.py:75
  1445.0 16.5 multiply_reduce_fusion.7
  1461.4 11.9 multiply_convert_fusion.3
  1484.3 24.0 reshape.200
  1508.3 15.4 fusion.216
  1549.2 11.3 broadcast_add_fusion.5
  1560.5 27.9 %add.339 = f32[1024,4096]{1,0:T(8,128)} reshape(f32[16,64,64,64]{3,2,1,0:T(8,128)} %broadcast_add_fusion.5) | data formatting | bytes 33554432 | tf_op jit(solution)/shard_map/while/body/eval_jaxpr/add | solution.py:75
  1588.4 16.5 multiply_reduce_fusion.7
  1604.9 11.9 multiply_convert_fusion.3
  1627.7 24.0 reshape.200
  1651.7 15.4 fusion.216
  1692.6 11.3 broadcast_add_fusion.5
  1704.0 27.9 %add.339 = f32[1024,4096]{1,0:T(8,128)} reshape(f32[16,64,64,64]{3,2,1,0:T(8,128)} %broadcast_add_fusion.5) | data formatting | bytes 33554432 | tf_op jit(solution)/shard_map/while/body/eval_jaxpr/add | solution.py:75
  1731.9 16.5 multiply_reduce_fusion.7
  1748.4 11.9 multiply_convert_fusion.3
  1771.2 24.0 reshape.200
  1795.1 15.4 fusion.216
  1836.0 11.3 broadcast_add_fusion.5
  1847.3 27.9 %add.339 = f32[1024,4096]{1,0:T(8,128)} reshape(f32[16,64,64,64]{3,2,1,0:T(8,128)} %broadcast_add_fusion.5) | data formatting | bytes 33554432 | tf_op jit(solution)/shard_map/while/body/eval_jaxpr/add | solution.py:75
  1875.2 16.5 multiply_reduce_fusion.7
  1891.7 11.9 multiply_convert_fusion.3
  1914.5 24.0 reshape.200
  1938.5 15.4 fusion.216
  1983.9 78.4 %reduce-scatter.24.cloned.1.call-done = f32[1024,2,320]{0,2,1:T(8,128)} async-done(((f32[4096,2,320]{0,2,1:T(8,128)}), f32[1024,2,320]{0,2,1:T(8,128)}) %reduce-scatter.24.cloned.1.call-update) | async-done | bytes 2621456 | tf_op jit(solution)/shard_map/reduce_scatter | solution.py:29
  2075.4 58.7 %all-gather.10.cloned.1.call-done = bf16[4096,1280]{1,0:T(8,128)(2,1)} async-done(((bf16[1024,1280]{1,0:T(8,128)(2,1)}), bf16[4096,1280]{1,0:T(8,128)(2,1)}) %all-gather.10.cloned.1.call-update) | async-done | bytes 10485776 | tf_op jit(solution)/shard_map/all_gather | solution.py:25
  2143.7 47.3 %all-gather.14.cloned.1.call-done = bf16[4096,3,320]{0,2,1:T(8,128)(2,1)} async-done(((bf16[1024,3,320]{0,2,1:T(8,128)(2,1)}), bf16[4096,3,320]{0,2,1:T(8,128)(2,1)}) %all-gather.14.cloned.1.call-update) | async-done | bytes 7864336 | tf_op jit(solution)/shard_map/all_gather | solution.py:25
  2207.0 12.8 fusion.105
  2249.7 23.3 all-reduce.13.cloned.1.call-done
  2280.9 88.2 %reduce-scatter.26.cloned.1.call-done = f32[1024,320]{0,1:T(8,128)} async-done(((f32[4096,320]{0,1:T(8,128)}), f32[1024,320]{0,1:T(8,128)}) %reduce-scatter.26.cloned.1.call-update) | async-done | bytes 1310736 | tf_op jit(solution)/shard_map/reduce_scatter | solution.py:33
  2378.0 87.5 %reduce-scatter.16.cloned.1.call-done = f32[1024,320]{0,1:T(8,128)} async-done(((f32[4096,320]{0,1:T(8,128)}), f32[1024,320]{0,1:T(8,128)}) %reduce-scatter.16.cloned.1.call-update) | async-done | bytes 1310736 | tf_op jit(solution)/shard_map/reduce_scatter | solution.py:33
  2469.9 19.1 all-reduce.1
  2489.0 106.0 %all-reduce.11.cloned.1.call-done = (f32[127,80]{0,1:T(8,128)}, f32[127,80]{0,1:T(8,128)}) async-done(((f32[127,80]{0,1:T(8,128)}, f32[127,80]{0,1:T(8,128)}), (f32[127,80]{0,1:T(8,128)}, f32[127,80]{0,1:T(8,128)})) %all-reduce.11.cloned.1.call-update) | async-done | bytes 81296 | tf_op jit(solution)/shard_map/psum | solution.py:274
  (325 shorter events, 428.0 us)
Async XLA Ops:
  7.2 822.7 %copy-start = (bf16[320,1280]{1,0:T(8,128)(2,1)S(1)}, bf16[320,1280]{1,0:T(8,128)(2,1)}, u32[]{:S(2)}) copy-start(bf16[320,1280]{1,0:T(8,128)(2,1)} %param.29) | copy-start | bytes 2457604
  7.2 211.2 %reduce-scatter.10.cloned.1.call-start = ((), (), s32[]{:S(2)}) async-start(), calls=%async_computation.13 | async-start | bytes 19660800 | tf_op jit(solution)/shard_map/reduce_scatter | solution.py:29
  97.9 126.5 %copy-start.53 = (bf16[127,80]{0,1:T(8,128)(2,1)S(1)}, bf16[127,80]{0,1:T(8,128)(2,1)}, u32[]{:S(2)}) copy-start(bf16[127,80]{0,1:T(8,128)(2,1)} %param.33) | copy-start | bytes 60964
  97.9 126.8 %copy-start.54 = (bf16[127,80]{0,1:T(8,128)(2,1)S(1)}, bf16[127,80]{0,1:T(8,128)(2,1)}, u32[]{:S(2)}) copy-start(bf16[127,80]{0,1:T(8,128)(2,1)} %param.34) | copy-start | bytes 60964
  97.9 166.7 %all-gather.6.cloned.1.call-start = ((), (), s32[]{:S(2)}) async-start(), calls=%async_computation.14 | async-start | bytes 6553600 | tf_op jit(solution)/shard_map/all_gather | solution.py:38
  224.0 377.3 %all-gather.8.cloned.1.call-start = ((), (), s32[]{:S(2)}) async-start(), calls=%async_computation.15 | async-start | bytes 3276800 | tf_op jit(solution)/shard_map/all_gather | solution.py:25
  224.4 45.7 %copy-start.51 = (s32[16]{0:T(128)}, s32[16]{0:T(128)S(1)}, u32[]{:S(2)}) copy-start(s32[16]{0:T(128)S(1)} %iota_add_fusion) | copy-start | bytes 196
  281.2 320.2 %copy-start.21 = (bf16[320,320]{1,0:T(8,128)(2,1)S(1)}, bf16[320,320]{1,0:T(8,128)(2,1)}, u32[]{:S(2)}) copy-start(bf16[320,320]{1,0:T(8,128)(2,1)} %param.23) | copy-start | bytes 614404
  575.6 31.4 %copy-start.17 = (bf16[1,1024,320]{1,2,0:T(8,128)(2,1)S(1)}, bf16[1,1024,320]{1,2,0:T(8,128)(2,1)}, u32[]{:S(2)}) copy-start(bf16[1,1024,320]{1,2,0:T(8,128)(2,1)} %param.35) | copy-start | bytes 1966084
  575.6 181.0 %reduce-scatter.12.cloned.1.call-start = ((), (), s32[]{:S(2)}) async-start(), calls=%async_computation.16 | async-start | bytes 6553600 | tf_op jit(solution)/shard_map/reduce_scatter | solution.py:33
  607.0 303.4 %reduce-scatter.18.cloned.1.call-start = ((), (), s32[]{:S(2)}) async-start(), calls=%async_computation.20 | async-start | bytes 26214400 | tf_op jit(solution)/shard_map/reduce_scatter | solution.py:29
  607.4 136.0 %copy-start.23 = (bf16[1280,320]{0,1:T(8,128)(2,1)S(1)}, bf16[1280,320]{0,1:T(8,128)(2,1)}, u32[]{:S(2)}) copy-start(bf16[1280,320]{0,1:T(8,128)(2,1)} %param.31) | copy-start | bytes 2457604
  753.4 3.2 copy-start.49
  753.4 12.0 copy-start.40
  753.4 12.0 copy-start.50
  753.4 312.7 %reduce-scatter.14.cloned.1.call-start = ((), (), s32[]{:S(2)}) async-start(), calls=%async_computation.17 | async-start | bytes 26214400 | tf_op jit(solution)/shard_map/reduce_scatter | solution.py:29
  765.4 502.8 %copy-start.28 = (f32[1024]{0:T(1024)}, f32[1024]{0:T(1024)S(1)}, u32[]{:S(2)}) copy-start(f32[1024]{0:T(1024)S(1)} %get-tuple-element.230) | copy-start | bytes 12292
  765.4 502.8 %copy-start.30 = (f32[1024]{0:T(1024)}, f32[1024]{0:T(1024)S(1)}, u32[]{:S(2)}) copy-start(f32[1024]{0:T(1024)S(1)} %get-tuple-element.231) | copy-start | bytes 12292
  839.8 226.4 %copy-start.42 = (f32[1280]{0:T(1024)S(1)}, f32[1280]{0:T(1024)}, u32[]{:S(2)}) copy-start(f32[1280]{0:T(1024)} %param.30) | copy-start | bytes 15364
  839.8 311.9 %all-gather.12.cloned.1.call-start = ((), (), s32[]{:S(2)}) async-start(), calls=%async_computation.21 | async-start | bytes 13107200 | tf_op jit(solution)/shard_map/all_gather | solution.py:25
  1081.4 176.9 %reduce-scatter.20.cloned.1.call-start = ((), (), s32[]{:S(2)}) async-start(), calls=%async_computation.22 | async-start | bytes 6553600 | tf_op jit(solution)/shard_map/reduce_scatter | solution.py:33
  1164.4 103.8 %copy-start.18 = (bf16[1,1024,320]{1,2,0:T(8,128)(2,1)S(1)}, bf16[1,1024,320]{1,2,0:T(8,128)(2,1)}, u32[]{:S(2)}) copy-start(bf16[1,1024,320]{1,2,0:T(8,128)(2,1)} %param.35) | copy-start | bytes 1966084
  1164.4 226.3 %reduce-scatter.22.cloned.1.call-start = ((), (), s32[]{:S(2)}) async-start(), calls=%async_computation.23 | async-start | bytes 6553600 | tf_op jit(solution)/shard_map/reduce_scatter | solution.py:29
  1268.1 63.5 %copy-start.36 = (f32[1024]{0:T(1024)}, f32[1024]{0:T(1024)S(1)}, u32[]{:S(2)}) copy-start(f32[1024]{0:T(1024)S(1)} %get-tuple-element.234) | copy-start | bytes 12292
  1268.2 63.5 %copy-start.38 = (f32[1024]{0:T(1024)}, f32[1024]{0:T(1024)S(1)}, u32[]{:S(2)}) copy-start(f32[1024]{0:T(1024)S(1)} %get-tuple-element.235) | copy-start | bytes 12292
  1338.8 723.5 %reduce-scatter.24.cloned.1.call-start = ((), (), s32[]{:S(2)}) async-start(), calls=%async_computation.24 | async-start | bytes 13107200 | tf_op jit(solution)/shard_map/reduce_scatter | solution.py:29
  1461.4 15.4 copy-start.2
  1476.8 3.8 copy-start.3
  1604.9 15.4 copy-start.2
  1620.3 3.8 copy-start.3
  1748.4 15.4 copy-start.2
  1763.7 3.8 copy-start.3
  1891.7 15.4 copy-start.2
  1907.1 3.8 copy-start.3
  1976.8 157.3 %all-gather.10.cloned.1.call-start = ((), (), s32[]{:S(2)}) async-start(), calls=%async_computation.18 | async-start | bytes 13107200 | tf_op jit(solution)/shard_map/all_gather | solution.py:25
  1983.8 80.4 %copy-start.27 = (bf16[4,1024,80]{1,2,0:T(8,128)(2,1)S(1)}, bf16[4,1024,80]{1,2,0:T(8,128)(2,1)}, u32[]{:S(2)}) copy-start(bf16[4,1024,80]{1,2,0:T(8,128)(2,1)} %get-tuple-element.132) | copy-start | bytes 1966084
  1983.8 207.1 %all-gather.14.cloned.1.call-start = ((), (), s32[]{:S(2)}) async-start(), calls=%async_computation.25 | async-start | bytes 9830400 | tf_op jit(solution)/shard_map/all_gather | solution.py:25
  2065.7 68.4 %copy-start.12 = (bf16[4,40,8,1024]{3,2,0,1:T(8,128)(2,1)S(1)}, bf16[4,40,8,1024]{3,2,0,1:T(8,128)(2,1)}, u32[]{:S(2)}) copy-start(bf16[4,40,8,1024]{3,2,0,1:T(8,128)(2,1)} %copy-done.11) | copy-start | bytes 7864324
  2065.7 207.3 %all-reduce.13.cloned.1.call-start = ((), (), s32[]{:S(2)}) async-start(), calls=%async_computation.28 | async-start | bytes 5242880 | tf_op jit(solution)/shard_map/psum | solution.py:285
  2134.2 7.3 copy-start.15
  2134.2 7.3 copy-start.20
  2141.5 49.5 %copy-start.16 = (bf16[4096,320,1]{0,1,2:T(8,128)(2,1)S(1)}, bf16[4096,320,1]{0,1,2:T(8,128)(2,1)}, u32[]{:S(2)}) copy-start(bf16[4096,320,1]{0,1,2:T(8,128)(2,1)} %reshape.190) | copy-start | bytes 7864324
  2143.7 54.2 %copy-start.25 = (bf16[320,3,320]{2,0,1:T(8,128)(2,1)S(1)}, bf16[320,3,320]{2,0,1:T(8,128)(2,1)}, u32[]{:S(2)}) copy-start(bf16[320,3,320]{2,0,1:T(8,128)(2,1)} %param.21) | copy-start | bytes 1843204
  2197.9 171.2 %reduce-scatter.26.cloned.1.call-start = ((), (), s32[]{:S(2)}) async-start(), calls=%async_computation.26 | async-start | bytes 6553600 | tf_op jit(solution)/shard_map/reduce_scatter | solution.py:33
  2205.9 259.7 %reduce-scatter.16.cloned.1.call-start = ((), (), s32[]{:S(2)}) async-start(), calls=%async_computation.19 | async-start | bytes 6553600 | tf_op jit(solution)/shard_map/reduce_scatter | solution.py:33
  2219.8 375.2 %all-reduce.11.cloned.1.call-start = ((), (), s32[]{:S(2)}) async-start(), calls=%async_computation.27 | async-start | bytes 163840 | tf_op jit(solution)/shard_map/psum | solution.py:274
  2222.0 5.6 copy-start.10
  2228.0 6.6 copy-start.52
  2241.8 127.3 %copy-start.6 = (bf16[1,1024,320]{1,2,0:T(8,128)(2,1)S(1)}, bf16[1,1024,320]{1,2,0:T(8,128)(2,1)}, u32[]{:S(2)}) copy-start(bf16[1,1024,320]{1,2,0:T(8,128)(2,1)} %param.20) | copy-start | bytes 1966084
  2241.8 127.3 %copy-start.33 = (f32[1024]{0:T(1024)S(1)}, f32[1024]{0:T(1024)}, u32[]{:S(2)}) copy-start(f32[1024]{0:T(1024)} %copy-done.32) | copy-start | bytes 12292
  2241.8 127.3 %copy-start.35 = (f32[1024]{0:T(1024)S(1)}, f32[1024]{0:T(1024)}, u32[]{:S(2)}) copy-start(f32[1024]{0:T(1024)} %copy-done.34) | copy-start | bytes 12292
  2241.8 127.3 %copy-start.44 = (f32[320]{0:T(512)S(1)}, f32[320]{0:T(512)}, u32[]{:S(2)}) copy-start(f32[320]{0:T(512)} %param.25) | copy-start | bytes 3844
  2241.8 223.7 %copy-start.4 = (f32[1024,320]{0,1:T(8,128)S(1)}, f32[1024,320]{0,1:T(8,128)}, u32[]{:S(2)}) copy-start(f32[1024,320]{0,1:T(8,128)} %get-tuple-element.219) | copy-start | bytes 3932164
  2241.8 223.7 %copy-start.19 = (bf16[1,1024,320]{1,2,0:T(8,128)(2,1)S(1)}, bf16[1,1024,320]{1,2,0:T(8,128)(2,1)}, u32[]{:S(2)}) copy-start(bf16[1,1024,320]{1,2,0:T(8,128)(2,1)} %param.35) | copy-start | bytes 1966084
  2241.9 223.7 %copy-start.29 = (f32[1024]{0:T(1024)S(1)}, f32[1024]{0:T(1024)}, u32[]{:S(2)}) copy-start(f32[1024]{0:T(1024)} %copy-done.28) | copy-start | bytes 12292
  2241.9 223.7 %copy-start.31 = (f32[1024]{0:T(1024)S(1)}, f32[1024]{0:T(1024)}, u32[]{:S(2)}) copy-start(f32[1024]{0:T(1024)} %copy-done.30) | copy-start | bytes 12292
  2241.9 223.7 %copy-start.37 = (f32[1024]{0:T(1024)S(1)}, f32[1024]{0:T(1024)}, u32[]{:S(2)}) copy-start(f32[1024]{0:T(1024)} %copy-done.36) | copy-start | bytes 12292
  2241.9 223.7 %copy-start.39 = (f32[1024]{0:T(1024)S(1)}, f32[1024]{0:T(1024)}, u32[]{:S(2)}) copy-start(f32[1024]{0:T(1024)} %copy-done.38) | copy-start | bytes 12292
  2241.9 223.7 %copy-start.41 = (f32[320]{0:T(512)S(1)}, f32[320]{0:T(512)}, u32[]{:S(2)}) copy-start(f32[320]{0:T(512)} %param.27) | copy-start | bytes 3844
  2241.9 223.7 %copy-start.48 = (f32[320]{0:T(512)S(1)}, f32[320]{0:T(512)}, u32[]{:S(2)}) copy-start(f32[320]{0:T(512)} %param.32) | copy-start | bytes 3844
  2273.1 6.6 copy-start.22
  2279.6 318.2 %copy-start.1 = (bf16[320,1280]{1,0:T(8,128)(2,1)S(1)}, bf16[320,1280]{1,0:T(8,128)(2,1)}, u32[]{:S(2)}) copy-start(bf16[320,1280]{1,0:T(8,128)(2,1)} %param.29) | copy-start | bytes 2457604
  2280.9 189.0 %copy-start.45 = (f32[320]{0:T(512)S(1)}, f32[320]{0:T(512)}, u32[]{:S(2)}) copy-start(f32[320]{0:T(512)} %get-tuple-element.141) | copy-start | bytes 3844
  2280.9 189.0 %copy-start.46 = (f32[320]{0:T(512)S(1)}, f32[320]{0:T(512)}, u32[]{:S(2)}) copy-start(f32[320]{0:T(512)} %get-tuple-element.147) | copy-start | bytes 3844
  (13 other events, 17.0 us)
Sparse Core Ops, SparseCore 0:
  98.0 120.2 reduce-scatter.9
  224.2 40.4 all-gather.5
  575.8 25.5 all-gather.7
  607.1 149.4 reduce-scatter.11
  759.1 151.2 reduce-scatter.17
  913.0 153.1 reduce-scatter.13
  1081.5 70.1 all-gather.11
  1164.5 93.7 reduce-scatter.19
  1338.9 51.7 reduce-scatter.21
  1976.9 85.2 reduce-scatter.23
  2063.9 70.1 all-gather.9
  2135.6 55.3 all-gather.13
  2198.0 75.0 all-reduce.12
  2275.2 93.7 reduce-scatter.25
  2371.2 94.2 reduce-scatter.15
  2471.6 123.3 all-reduce.10
